TPU v7x, 768 devices: a whole 4x8x12 slice. The times are simulated.
768 devices in a mesh: dp: 32 (over y, z_hi, core), segment: 24 (over x, z_lo).
Axes of the slice: x: 4, y: 8, z: 12 (z_hi: 2, z_lo: 6; z = z_hi * 6 + z_lo), core: 2. Of those that a mesh axis runs over, the one named last changes fastest.
Arguments:
- inputs: bfloat16 [24, 32, 256, 1024], P('segment', 'dp'), may hold values from -6 to 6
- values: bfloat16 [24, 32, 256, 1024], P('segment', 'dp'), may hold values from -6 to 6
- gate_values: bfloat16 [24, 32, 256, 1024], P('segment', 'dp'), may hold values from -6 to 6
- out_grad: bfloat16 [24, 32, 256, 1024], P('segment', 'dp'), may hold values from -6 to 6
- lengths: int32 [24, 32], P('segment', 'dp'), may hold values from 32 to 256, as said below
- qk_weight: bfloat16 [24, 1024, 2048], P('segment', 'dp'), may hold values from -0.1875 to 0.1875
Outputs:
- grad_inputs: bfloat16 [24, 32, 256, 1024], P('segment', 'dp')
- grad_values: bfloat16 [24, 32, 256, 1024], P('segment', 'dp')
- grad_gates: bfloat16 [24, 32, 256, 1024], P('segment', 'dp')
- grad_weight: float32 [24, 1024, 2048], P('segment', 'dp')
Inputs may be any that keep to these rules, and one draw needn't show every extreme that they name: `lengths`: in every layer some sequence has the full length 256.
All inputs are finite; a program needn't handle non-finite values.
Results may differ from a plain program's by a relative error of at most 0.025.
Values may be sent and summed in bfloat16 or wider, within the bound.
A program may use at most 64 MiB of HBM per device.

v0:
```python
import jax
import jax.numpy as jnp
from jax import lax
from jax.sharding import PartitionSpec as P

H = 8
DH = 128


def from_behind(x, axis, by):
    count = lax.axis_size(axis)
    return lax.ppermute(x, axis, [(i, (i + by) % count) for i in range(count)])


def window(qk_pre, values, gate_values, length):
    seq_len = qk_pre.shape[0]
    qk_act = jax.nn.silu(qk_pre).astype(jnp.bfloat16)
    queries = qk_act[:, : H * DH].reshape(seq_len, H, DH)
    keys = qk_act[:, H * DH :].reshape(seq_len, H, DH)
    scores = jnp.einsum("ihd,jhd->hij", queries, keys, preferred_element_type=jnp.float32) * DH ** (
        -0.5
    )
    row_ids = lax.broadcasted_iota(jnp.int32, (seq_len, seq_len), 0)
    col_ids = lax.broadcasted_iota(jnp.int32, (seq_len, seq_len), 1)
    valid = (col_ids <= row_ids) & (row_ids < length)
    attention = jnp.where(valid[None], jax.nn.silu(scores), 0.0).astype(jnp.bfloat16)
    heads_values = values.reshape(seq_len, H, DH)
    mixed_heads = jnp.einsum(
        "hij,jhd->ihd", attention, heads_values, preferred_element_type=jnp.float32
    ).reshape(seq_len, H * DH)
    row_mean = jnp.mean(mixed_heads, axis=-1, keepdims=True)
    centered = mixed_heads - row_mean
    variance = jnp.mean(centered * centered, axis=-1, keepdims=True)
    normed = centered * lax.rsqrt(variance + 1e-05)
    live = (lax.broadcasted_iota(jnp.int32, (seq_len, 1), 0) < length).astype(jnp.float32)
    return normed * gate_values.astype(jnp.float32) * live


def on_device(inputs, values, gate_values, out_grad, lengths, qk_weight):
    tokens_in = inputs[0, 0]
    seq_values = values[0, 0]
    seq_gates = gate_values[0, 0]
    length = lengths[0, 0]
    shard_weight = qk_weight[0]
    full_weight = lax.all_gather(shard_weight, "dp", axis=0, tiled=True)
    pre = jnp.dot(tokens_in, full_weight, preferred_element_type=jnp.float32)
    incoming = from_behind(out_grad[0, 0], "segment", -1)
    outcome, pullback = jax.vjp(lambda a, b, c: window(a, b, c, length), pre, seq_values, seq_gates)
    grad_pre, grad_val, grad_gate = pullback(incoming.astype(jnp.float32))
    grad_pre_b = grad_pre.astype(jnp.bfloat16)
    grad_in = lax.dot_general(
        grad_pre_b, full_weight, (((1,), (1,)), ((), ())), preferred_element_type=jnp.float32
    ).astype(jnp.bfloat16)
    term = lax.dot_general(
        tokens_in, grad_pre_b, (((0,), (0,)), ((), ())), preferred_element_type=jnp.float32
    )
    grad_shard = lax.psum_scatter(
        term.astype(jnp.bfloat16), "dp", scatter_dimension=0, tiled=True
    ).astype(jnp.float32)
    return (grad_in[None, None], grad_val[None, None], grad_gate[None, None], grad_shard[None])


def solution(mesh):
    return jax.shard_map(
        on_device,
        mesh=mesh,
        in_specs=(
            P("segment", "dp", None, None),
            P("segment", "dp", None, None),
            P("segment", "dp", None, None),
            P("segment", "dp", None, None),
            P("segment", "dp"),
            P("segment", "dp", None),
        ),
        out_specs=(
            P("segment", "dp", None, None),
            P("segment", "dp", None, None),
            P("segment", "dp", None, None),
            P("segment", "dp", None),
        ),
        check_vma=False,
    )
```

profile of v0, /device:TPU:1, one launch (start us, length us, event | category | flops | bytes accessed | tf_op | source)
XLA Modules:
  0.0 349.6 jit_solution(13073080869072004821)
XLA Ops:
  7.2 0.0 copy-start
  7.2 0.0 all-gather.3.cloned.1.call-start
  7.2 0.7 all-gather.3.cloned.1.call-update
  7.9 0.0 reduce-scatter.4.cloned.1.call-start
  8.0 15.5 %collective-permute-start = (bf16[256,1024]{1,0:T(8,128)(2,1)}, bf16[256,1024]{1,0:T(8,128)(2,1)}, u32[]{:S(2)}, u32[]{:S(2)}) collective-permute-start(bf16[256,1024]{1,0:T(8,128)(2,1)} %bitcast.86), channel_id=1, source_target_pairs={{0,23},{1,0},{2,1},{3,2},{4,3},{5,4},{6,5},{7,6},{8,7},{9,8},{10,9... | collective-permute-start | bytes 1572872 | tf_op jit(solution)/shard_map/ppermute | solution.py:12
  24.1 1.1 copy.44
  25.2 0.0 copy-start.4
  25.3 0.1 fusion.24
  25.4 122.4 %all-gather.3.cloned.1.call-done = bf16[1,1024,2048]{2,1,0:T(8,128)(2,1)} async-done(((bf16[1,32,2048]{2,1,0:T(8,128)(2,1)}), bf16[1,1024,2048]{2,1,0:T(8,128)(2,1)}) %all-gather.3.cloned.1.call-update) | async-done | bytes 4194320 | tf_op jit(solution)/shard_map/all_gather | solution.py:45
  147.8 4.8 %multiply_convert_fusion = (bf16[256,2048]{1,0:T(8,128)(2,1)S(1)}, f32[256,2048]{1,0:T(8,128)}) fusion(bf16[1,1024,2048]{2,1,0:T(8,128)(2,1)} %all-gather.3.cloned.1.call-done, bf16[1,1,256,1024]{3,2,1,0:T(8,128)(2,1)S(1)} %copy-done), kind=kOutput, calls=%fused_computation.17 | convolution fusion | flops 1076363264 | bytes 7864320 | tf_op jit(solution)/shard_map/dot_general | solution.py:46
  152.6 0.1 fusion.30
  152.7 0.2 copy.42
  152.9 0.0 copy-start.6
  152.9 0.2 copy.43
  153.1 0.0 copy-start.8
  153.1 2.1 select_convert_fusion
  155.2 0.5 fusion.31
  155.7 0.0 copy-start.3
  155.8 0.4 copy-done.1
  156.2 0.3 copy.26
  156.6 0.2 fusion.17
  156.7 0.0 collective-permute-done
  156.7 0.1 copy-done.3
  156.8 1.5 multiply_reduce_fusion
  158.3 2.4 fusion.29
  160.7 0.1 broadcast_add_fusion
  160.8 0.2 copy.37
  161.0 0.7 copy-done.5
  161.7 2.9 fusion.9
  164.6 0.0 copy-done.9
  164.6 0.0 copy-start.7
  164.6 0.5 fusion.32
  165.1 0.5 copy-done.7
  165.7 0.3 fusion.33
  166.0 0.2 copy.39
  166.2 0.2 copy.38
  166.4 0.0 copy-start.10
  166.4 5.7 %convert_bitcast_fusion = bf16[1024,2048]{0,1:T(8,128)(2,1)} fusion(bf16[1,1,256,1024]{3,2,1,0:T(8,128)(2,1)S(1)} %copy-done, f32[256,2048]{1,0:T(8,128)} %get-tuple-element.20, bf16[256,1024]{1,0:T(8,128)(2,1)S(1)} %copy.39, bf16[256,1024]{1,0:T(8,128)(2,1)S(1)} %copy.38), kind=kOutput, calls=%fused_computation.4 | convolution fusion | flops 1083179008 | bytes 7864320 | tf_op jit(solution)/shard_map/dot_general | solution.py:54
  172.1 6.5 %copy.40 = bf16[1024,2048]{1,0:T(8,128)(2,1)} copy(bf16[1024,2048]{0,1:T(8,128)(2,1)} %convert_bitcast_fusion) | data formatting | bytes 8388608
  178.7 0.0 reduce-scatter.4.cloned.1.call-update
  178.7 1.2 copy-done.2
  179.9 0.3 fusion.34
  180.2 1.0 copy.34
  181.2 5.4 %fusion.13 = bf16[1,1,256,1024]{3,2,1,0:T(8,128)(2,1)} fusion(bf16[1,1024,2048]{2,1,0:T(8,128)(2,1)} %all-gather.3.cloned.1.call-done, f32[256,2048]{1,0:T(8,128)} %get-tuple-element.20, bf16[256,1024]{1,0:T(8,128)(2,1)S(1)} %copy.39, bf16[256,1024]{1,0:T(8,128)(2,1)} %copy-done.10), kind=kOutput, calls=%fused_computation.25 | convolution fusion | flops 1081344000 | bytes 7864320 | tf_op jit(solution)/shard_map/dot_general | solution.py:51
  186.7 153.8 %reduce-scatter.4.cloned.1.call-done = bf16[32,2048]{1,0:T(8,128)(2,1)} async-done(((bf16[1024,2048]{1,0:T(8,128)(2,1)}), bf16[32,2048]{1,0:T(8,128)(2,1)}) %reduce-scatter.4.cloned.1.call-update) | async-done | bytes 131088
  340.5 1.2 copy.41
  341.6 0.1 bitcast_convert_fusion
  341.7 1.0 copy.35
  (14 shorter events, 0.0 us)
Async XLA Ops:
  7.2 140.6 %copy-start = (bf16[1,1,256,1024]{3,2,1,0:T(8,128)(2,1)S(1)}, bf16[1,1,256,1024]{3,2,1,0:T(8,128)(2,1)}, u32[]{:S(2)}) copy-start(bf16[1,1,256,1024]{3,2,1,0:T(8,128)(2,1)} %param.6) | copy-start | bytes 1572868
  7.2 140.6 %all-gather.3.cloned.1.call-start = ((), (), s32[]{:S(2)}) async-start(), calls=%async_computation.1 | async-start | bytes 4325376 | tf_op jit(solution)/shard_map/all_gather | solution.py:45
  7.9 332.5 %reduce-scatter.4.cloned.1.call-start = ((), (), s32[]{:S(2)}) async-start(), calls=%async_computation.2 | async-start | bytes 4325376
  8.0 148.8 %collective-permute-start = (bf16[256,1024]{1,0:T(8,128)(2,1)}, bf16[256,1024]{1,0:T(8,128)(2,1)}, u32[]{:S(2)}, u32[]{:S(2)}) collective-permute-start(bf16[256,1024]{1,0:T(8,128)(2,1)} %bitcast.86), channel_id=1, source_target_pairs={{0,23},{1,0},{2,1},{3,2},{4,3},{5,4},{6,5},{7,6},{8,7},{9,8},{10,9... | collective-permute-start | bytes 1572872 | tf_op jit(solution)/shard_map/ppermute | solution.py:12
  25.2 130.0 %copy-start.4 = (bf16[32,8,8,128]{3,2,1,0:T(8,128)(2,1)}, bf16[32,8,8,128]{3,2,1,0:T(8,128)(2,1)S(1)}, u32[]{:S(2)}) copy-start(bf16[32,8,8,128]{3,2,1,0:T(8,128)(2,1)S(1)} %copy.44) | copy-start | bytes 1572868
  152.9 2.4 copy-start.6
  153.1 2.1 copy-start.8
  155.2 1.0 copy-start.1
  155.7 1.0 copy-start.3
  160.7 1.0 copy-start.5
  161.7 2.9 copy-start.9
  164.6 1.0 copy-start.7
  166.4 5.7 %copy-start.10 = (bf16[256,1024]{1,0:T(8,128)(2,1)}, bf16[256,1024]{1,0:T(8,128)(2,1)S(1)}, u32[]{:S(2)}) copy-start(bf16[256,1024]{1,0:T(8,128)(2,1)S(1)} %copy.38) | copy-start | bytes 1572868
  178.7 1.2 copy-start.2
Sparse Core Ops, SparseCore 0:
  11.9 135.7 all-gather.2
  178.8 161.6 reduce-scatter.3
where the time goes:
time: 354 us; the launch traced here: 350 us
  waiting for transfers between devices  277 us (78%)
  matrix products  22.6 us (6%)
  starting transfers between devices  15.5 us (4%)
  local copies, waits for them, and re-layouts  15.3 us (4%)
  between operations  14.9 us (4%)
  other arithmetic  4.35 us (1%)
    unnamed x3, waiting for transfers between devices  155 us
    all_gather x1, waiting for transfers between devices, on_device(): full_weight = lax.all_gather(shard_weight, 'dp', axis=0, tiled=True)  122 us
    ppermute x1, starting transfers between devices, from_behind(): return lax.ppermute(x, axis, [(i, (i + by) % count) for i in range(count)])  15.5 us
    unnamed x27, local copies, waits for them, and re-layouts  13.8 us
  transfers between devices with their start and end apart: 3, of which 2 were waited for; matrix products, arithmetic and copies ran while one was open for 5% of the time, Pallas kernels for 0%

commit v1 on v0

v1 whole, which is shorter than its diff:
```python
import jax
import jax.numpy as jnp
from jax import lax
from jax.experimental import pallas as pl
from jax.experimental.pallas import tpu as pltpu
from jax.sharding import PartitionSpec as P

MESH = pl.DeviceIdType.MESH
H = 8
DH = 128
L = 256
D = 1024
SCALE = DH ** (-0.5)
Y = 8
Z_LO = 6
Z = 12
NG = 4
F32 = jnp.float32
BF16 = jnp.bfloat16

NT = (((1,), (1,)), ((), ()))
TN = (((0,), (0,)), ((), ()))


def dot(a, b, dims=(((1,), (0,)), ((), ()))):
    return lax.dot_general(a, b, dims, preferred_element_type=F32)


def sigmoid(v):
    return 0.5 * jnp.tanh(0.5 * v) + 0.5


def kernel(
    x_hbm,
    v_hbm,
    g_hbm,
    og_hbm,
    len_ref,
    w_hbm,
    gi_hbm,
    gv_hbm,
    gg_hbm,
    gw_hbm,
    wb,
    xv,
    vv,
    gt,
    ct,
    xt,
    mask,
    dact,
    qk,
    dsc,
    at,
    mx,
    dm,
    gp,
    gpw,
    gx,
    tm,
    sb,
    rb,
    za,
    zs,
    zr,
    fb,
    gwb,
    gib,
    ggb,
    gvb,
    l_sem,
    o_sem,
    ag_s,
    ag_r,
    az_s,
    az_r,
    ad_s,
    ad_r,
    m_s,
    m_r,
    ex_s,
    ex_r,
    rs_s,
    rs_r,
    rz_s,
    rz_r,
    rf_s,
    rf_r,
):
    d = lax.axis_index("dp")
    seg = lax.axis_index("segment")
    nseg = lax.axis_size("segment")
    c = lax.rem(d, 2)
    zh = lax.rem(lax.div(d, 2), 2)
    y = lax.div(d, 4)

    def ring(i):
        return lax.rem(i + 2 * Y, Y)

    def dp_of(yy, zz, cc):
        return (yy * 2 + zz) * 2 + cc

    sib = {"dp": dp_of(y, zh, 1 - c)}
    opp = {"dp": dp_of(y, 1 - zh, c)}
    nxt = {1: {"dp": dp_of(ring(y + 1), zh, c)}, -1: {"dp": dp_of(ring(y - 1), zh, c)}}
    behind = {"segment": lax.rem(seg + nseg - 1, nseg)}
    ahead = {"segment": lax.rem(seg + 1, nseg)}

    barrier = pltpu.get_barrier_semaphore()
    for peer in (nxt[1], nxt[-1], sib, opp, behind, ahead):
        pl.semaphore_signal(barrier, inc=1, device_id=peer, device_id_type=MESH)

    def remote(src, dst, s, r, dev):
        return pltpu.make_async_remote_copy(
            src_ref=src, dst_ref=dst, send_sem=s, recv_sem=r, device_id=dev, device_id_type=MESH
        )

    stage = []
    for g in range(NG):
        for half in range(2):
            stage.append(
                pltpu.make_async_copy(
                    w_hbm.at[:, pl.ds(half * D + g * 256, 256)],
                    wb.at[g, y, zh, c, :, pl.ds(half * 256, 256)],
                    l_sem.at[2 * g + half],
                )
            )
    for cp in stage:
        cp.start()
    loads = [
        pltpu.make_async_copy(x_hbm, xv.at[0], l_sem.at[8]),
        pltpu.make_async_copy(v_hbm, vv, l_sem.at[9]),
        pltpu.make_async_copy(g_hbm, gt, l_sem.at[10]),
    ]
    for cp in loads:
        cp.start()
    for cp in stage:
        cp.wait()
    pl.semaphore_wait(barrier, 6)

    sent = []

    def start(cp):
        cp.start()
        sent.append(cp)

    def ag_ref(g, yy, zz, dr, step):
        if step == 4:
            return wb.at[g, yy, zz, c, pl.ds(0 if dr == 1 else 16, 16)]
        return wb.at[g, yy, zz, c]

    def ag(unit, dr, step, back):
        part, g = divmod(unit, NG)
        zz = zh if part == 0 else 1 - zh
        ref = ag_ref(g, ring(y - dr * (step - 1 + back)), zz, dr, step)
        di = 0 if dr == 1 else 1
        return remote(ref, ref, ag_s.at[unit, di, step - 1], ag_r.at[unit, di, step - 1], nxt[dr])

    def az(g, zz):
        ref = wb.at[g, y, zz, c]
        return remote(ref, ref, az_s.at[g], az_r.at[g], opp)

    def ad(unit, cc):
        part, g = divmod(unit, NG)
        zz = zh if part == 0 else 1 - zh
        ref = wb.at[g, :, zz, cc]
        return remote(ref, ref, ad_s.at[unit], ad_r.at[unit], sib)

    def issue(unit):
        if unit >= NG:
            az(unit - NG, 1 - zh).wait_recv()
        for dr in (1, -1):
            start(ag(unit, dr, 1, 0))

    for g in range(NG):
        issue(g) if g < 2 else None
        start(az(g, zh))
    swap_x = remote(x_hbm, xv.at[1], m_s.at[0], m_r.at[0], sib)
    start(swap_x)
    shift = remote(og_hbm, ct, m_s.at[1], m_r.at[1], behind)

    rows = lax.broadcasted_iota(jnp.int32, (L, L), 0)
    cols = lax.broadcasted_iota(jnp.int32, (L, L), 1)
    length = len_ref[0, 0]
    mask[...] = jnp.where((cols <= rows) & (rows < length), 1.0, 0.0)
    loads[0].wait()
    loads[1].wait()

    def forward(g):
        wg = wb[g].reshape(D, 512)
        pre = dot(xv[0], wg)
        sg = sigmoid(pre)
        act = pre * sg
        dact[g] = sg + act - act * sg
        actb = act.astype(BF16)
        qk[g] = actb
        for hh in range(2):
            h = 2 * g + hh
            q = actb[:, hh * DH : (hh + 1) * DH]
            k = actb[:, 256 + hh * DH : 256 + (hh + 1) * DH]
            s = dot(q, k, NT) * SCALE
            ss = sigmoid(s)
            sa = s * ss
            m = mask[...]
            att = (sa * m).astype(BF16)
            at[h] = att
            dsc[h] = (ss + sa - sa * ss) * (m * SCALE)
            mx[:, h * DH : (h + 1) * DH] = dot(att, vv[:, h * DH : (h + 1) * DH])

    for t in range(1, 2 * NG + 4):
        if t + 1 < 2 * NG:
            issue(t + 1)
        if t == 2:
            start(shift)
            xt[:, 0:L] = xv[0].T
        if t == 5:
            swap_x.wait_recv()
            xt[:, L : 2 * L] = xv[1].T
        unit = t - 4
        if 0 <= unit < 2 * NG:
            for dr in (1, -1):
                ag(unit, dr, 4, 1).wait_recv()
            start(ad(unit, c))
        for step in (3, 2, 1):
            unit = t - step
            if 0 <= unit < 2 * NG:
                for dr in (1, -1):
                    ag(unit, dr, step, 1).wait_recv()
                    start(ag(unit, dr, step + 1, 0))
        g = t - 4 - NG
        if g >= 0:
            ad(g, 1 - c).wait_recv()
            ad(NG + g, 1 - c).wait_recv()
            forward(g)

    loads[2].wait()
    shift.wait_recv()
    RB = 32

    @pl.loop(0, L // RB)
    def _(i):
        sl = pl.ds(pl.multiple_of(i * RB, RB), RB)
        mixed = mx[sl, :]
        cen = mixed - jnp.sum(mixed, axis=-1, keepdims=True) * (1.0 / D)
        var = jnp.sum(cen * cen, axis=-1, keepdims=True) * (1.0 / D)
        r = lax.rsqrt(var + 1e-05)
        normed = cen * r
        row = lax.broadcasted_iota(jnp.int32, (RB, 1), 0) + i * RB
        live = jnp.where(row < length, 1.0, 0.0)
        cot = ct[sl, :].astype(F32) * live
        ggb[sl, :] = (cot * normed).astype(BF16)
        dn = cot * gt[sl, :].astype(F32)
        m1 = jnp.sum(dn, axis=-1, keepdims=True) * (1.0 / D)
        m2 = jnp.sum(dn * normed, axis=-1, keepdims=True) * (1.0 / D)
        dm[sl, :] = (r * (dn - m1 - normed * m2)).astype(BF16)

    outs = [pltpu.make_async_copy(ggb, gg_hbm, o_sem.at[0])]
    outs[0].start()

    def swap(h, half):
        return remote(gp.at[h, half], gx.at[h], ex_s.at[h], ex_r.at[h], sib)

    def backward(h):
        g, hh = divmod(h, 2)
        cq = slice(hh * DH, (hh + 1) * DH)
        ck = slice(256 + hh * DH, 256 + (hh + 1) * DH)
        ch = slice(h * DH, (h + 1) * DH)
        datt = dot(dm[:, ch], vv[:, ch], NT).astype(BF16).astype(F32)
        ds = (datt * dsc[h]).astype(BF16)
        dq = dot(ds, qk[g, :, ck]).astype(BF16).astype(F32)
        dq = (dq * dact[g, :, cq]).astype(BF16)
        dk = dot(ds, qk[g, :, cq], TN).astype(BF16).astype(F32)
        dk = (dk * dact[g, :, ck]).astype(BF16)
        gp[h, 0] = dq
        gp[h, 1] = dk
        gpw[g, :, cq] = dq
        gpw[g, :, ck] = dk
        start(swap(h, 1 - c))

    def term(h):
        swap(h, 1 - c).wait_recv()
        full = dot(xt[:, 0:L], gp[h, c]) + dot(xt[:, L : 2 * L], gx[h])
        tm[h] = full.reshape(Y, 128, DH)

    def rs(h, dr, step):
        di = 0 if dr == 1 else 1
        src, dst = sb.at[h, di, step - 1], rb.at[h, di, step - 1]
        if step == 1:
            src, dst = src.at[pl.ds(0, 64)], dst.at[pl.ds(0, 64)]
        return remote(src, dst, rs_s.at[h, di, step - 1], rs_r.at[h, di, step - 1], nxt[dr])

    def rs_send(h, dr, step):
        di = 0 if dr == 1 else 1
        yy = ring(y + dr * (5 - step))
        lo, hi = (0, 64) if dr == 1 else (64, 0)
        if step == 1:
            sb[h, di, 0, 0:64] = tm[h, yy, lo : lo + 64].astype(BF16)
        elif step == 2:
            sb[h, di, 1, lo : lo + 64] = (tm[h, yy, lo : lo + 64] + rb[h, di, 0, 0:64].astype(F32)).astype(BF16)
            sb[h, di, 1, hi : hi + 64] = tm[h, yy, hi : hi + 64].astype(BF16)
        else:
            sb[h, di, step - 1] = (tm[h, yy] + rb[h, di, step - 2].astype(F32)).astype(BF16)
        start(rs(h, dr, step))

    def rz(h):
        return remote(zs.at[h], zr.at[h], rz_s.at[h], rz_r.at[h], opp)

    def rs_end(h):
        for dr in (1, -1):
            rs(h, dr, 4).wait_recv()
        full = tm[h, y] + rb[h, 0, 3].astype(F32) + rb[h, 1, 3].astype(F32)
        za[h] = full.reshape(2, 64, DH)
        zs[h] = za[h, 1 - zh].astype(BF16)
        start(rz(h))

    def col(h, cc):
        return pl.ds(pl.multiple_of(cc * D + h * DH, DH), DH)

    def rf(h, cc):
        return remote(fb.at[h, 1 - c], gwb.at[:, col(h, cc)], rf_s.at[h], rf_r.at[h], sib)

    def z_end(h):
        rz(h).wait_recv()
        full = za[h, zh] + zr[h].astype(F32)
        fb[h] = full.reshape(2, 32, DH)
        start(rf(h, c))
        gwb[:, col(h, c)] = fb[h, c]

    def grad_values(h):
        ch = slice(h * DH, (h + 1) * DH)
        gvb[:, ch] = dot(at[h], dm[:, ch], TN).astype(BF16)

    def grad_inputs(n):
        acc = dot(gpw[0], wb[0, 2 * n : 2 * n + 2].reshape(256, 512), NT)
        for g in range(1, NG):
            acc = acc + dot(gpw[g], wb[g, 2 * n : 2 * n + 2].reshape(256, 512), NT)
        gib[:, n * 256 : (n + 1) * 256] = acc.astype(BF16)

    Z_LAG = 3
    backward(0)
    for t in range(0, H + 4 + Z_LAG):
        if t + 1 < H:
            backward(t + 1)
        if t < H:
            term(t)
            for dr in (1, -1):
                rs_send(t, dr, 1)
        for step in (3, 2, 1):
            h = t - step
            if 0 <= h < H:
                for dr in (1, -1):
                    rs(h, dr, step).wait_recv()
                    rs_send(h, dr, step + 1)
        h = t - 4
        if 0 <= h < H:
            rs_end(h)
        if t < H:
            grad_values(t)
            if t == H - 1:
                outs.append(pltpu.make_async_copy(gvb, gv_hbm, o_sem.at[1]))
                outs[-1].start()
        elif t < H + 4:
            grad_inputs(t - H)
            if t == H + 3:
                outs.append(pltpu.make_async_copy(gib, gi_hbm, o_sem.at[2]))
                outs[-1].start()
        h = t - 4 - Z_LAG
        if 0 <= h < H:
            z_end(h)
    for h in range(H):
        rf(h, 1 - c).wait_recv()
    outs.append(pltpu.make_async_copy(gwb, gw_hbm, o_sem.at[3]))
    outs[-1].start()
    for cp in sent:
        cp.wait_send()
    for cp in outs:
        cp.wait()


def fused(x, v, g, og, lengths, w):
    any_space = pl.BlockSpec(memory_space=pl.ANY)
    dma = pltpu.SemaphoreType.DMA
    seq = (L, D)
    return pl.pallas_call(
        kernel,
        out_shape=(
            jax.ShapeDtypeStruct(seq, BF16),
            jax.ShapeDtypeStruct(seq, BF16),
            jax.ShapeDtypeStruct(seq, BF16),
            jax.ShapeDtypeStruct((32, 2 * D), F32),
        ),
        in_specs=[any_space] * 4 + [pl.BlockSpec(memory_space=pltpu.SMEM), any_space],
        out_specs=(any_space,) * 4,
        scratch_shapes=[
            pltpu.VMEM((NG, Y, 2, 2, 32, 512), BF16),
            pltpu.VMEM((2, L, D), BF16),
            pltpu.VMEM(seq, BF16),
            pltpu.VMEM(seq, BF16),
            pltpu.VMEM(seq, BF16),
            pltpu.VMEM((D, 2 * L), BF16),
            pltpu.VMEM((L, L), F32),
            pltpu.VMEM((NG, L, 512), F32),
            pltpu.VMEM((NG, L, 512), BF16),
            pltpu.VMEM((H, L, L), F32),
            pltpu.VMEM((H, L, L), BF16),
            pltpu.VMEM(seq, F32),
            pltpu.VMEM(seq, BF16),
            pltpu.VMEM((H, 2, L, DH), BF16),
            pltpu.VMEM((NG, L, 512), BF16),
            pltpu.VMEM((H, L, DH), BF16),
            pltpu.VMEM((H, Y, 128, DH), F32),
            pltpu.VMEM((H, 2, 4, 128, DH), BF16),
            pltpu.VMEM((H, 2, 4, 128, DH), BF16),
            pltpu.VMEM((H, 2, 64, DH), F32),
            pltpu.VMEM((H, 64, DH), BF16),
            pltpu.VMEM((H, 64, DH), BF16),
            pltpu.VMEM((H, 2, 32, DH), F32),
            pltpu.VMEM((32, 2 * D), F32),
            pltpu.VMEM(seq, BF16),
            pltpu.VMEM(seq, BF16),
            pltpu.VMEM(seq, BF16),
            dma((11,)),
            dma((4,)),
            dma((2 * NG, 2, 4)),
            dma((2 * NG, 2, 4)),
            dma((NG,)),
            dma((NG,)),
            dma((2 * NG,)),
            dma((2 * NG,)),
            dma((2,)),
            dma((2,)),
            dma((H,)),
            dma((H,)),
            dma((H, 2, 4)),
            dma((H, 2, 4)),
            dma((H,)),
            dma((H,)),
            dma((H,)),
            dma((H,)),
        ],
        compiler_params=pltpu.CompilerParams(
            collective_id=0, has_side_effects=True, vmem_limit_bytes=60 * 1024 * 1024
        ),
        name="fused",
    )(x, v, g, og, lengths, w)


def on_device(inputs, values, gate_values, out_grad, lengths, qk_weight):
    gi, gv, gg, gw = fused(
        inputs[0, 0], values[0, 0], gate_values[0, 0], out_grad[0, 0], lengths, qk_weight[0]
    )
    return (gi[None, None], gv[None, None], gg[None, None], gw[None])


def solution(mesh):
    seq = P("segment", "dp", None, None)
    return jax.shard_map(
        on_device,
        mesh=mesh,
        in_specs=(seq, seq, seq, seq, P("segment", "dp"), P("segment", "dp", None)),
        out_specs=(seq, seq, seq, P("segment", "dp", None)),
        check_vma=False,
    )
```

time: 354 us -> 125 us (0.35); the launches traced: 350 us -> 125 us
  waiting for transfers between devices: 277 us -> 0 us
  Pallas kernels: 0 us -> 119 us
  matrix products: 22.6 us -> 0 us
  starting transfers between devices: 15.5 us -> 0 us
  between operations: 14.9 us -> 1.3 us
  local copies, waits for them, and re-layouts: 15.3 us -> 4.95 us
  other arithmetic: 4.35 us -> 0 us
    unnamed x3 -> x0, waiting for transfers between devices: 155 us -> none
    all_gather x1 -> x0, waiting for transfers between devices: 122 us -> none  [on_device(): full_weight = lax.all_gather(shard_weight, 'dp', axis=0, tiled=True)]
    pallas_call x0 -> x1, Pallas kernels: none -> 119 us  [fused(): pl.pallas_call(kernel, out_shape=(jax.ShapeDtypeStruct(seq, BF16), jax.Sh...]
    dot_general x9 -> x0, matrix products: 22.6 us -> none  [the longest x1 5.72 us: on_device(): lax.dot_general(tokens_in, grad_pre_b, (((0,), (0,)), ((), ())), preferre...]
    ppermute x1 -> x0, starting transfers between devices: 15.5 us -> none  [from_behind(): return lax.ppermute(x, axis, [(i, (i + by) % count) for i in range(count)])]
    unnamed x27 -> x10, local copies, waits for them, and re-layouts: 13.8 us -> 4.95 us
    reduce_sum x3 -> x0, other arithmetic: 4.02 us -> none  [the longest x1 2.39 us: window(): centered = mixed_heads - row_mean]
  transfers between devices with their start and end apart: 3 -> 0, of which waited for: 2 -> 0; matrix products, arithmetic and copies ran while one was open for 5% -> 0% of each run, Pallas kernels for 0% -> 0%
where the time goes in v1:
time: 125 us
  Pallas kernels  119 us (95%)
  local copies, waits for them, and re-layouts  4.95 us (4%)
  between operations  1.3 us (1%)
    pallas_call x1, Pallas kernels, fused(): pl.pallas_call(kernel, out_shape=(jax.ShapeDtypeStruct(seq, BF16), jax.Sh...  119 us
    unnamed x10, local copies, waits for them, and re-layouts  4.95 us

profile of v1, /device:TPU:1, one launch (start us, length us, event | category | flops | bytes accessed | tf_op | source)
XLA Modules:
  0.0 124.8 jit_solution(12334523908370763524)
XLA Ops:
  1.3 118.5 %fused.1 = (bf16[256,1024]{1,0:T(8,128)(2,1)}, bf16[256,1024]{1,0:T(8,128)(2,1)}, bf16[256,1024]{1,0:T(8,128)(2,1)}, f32[32,2048]{1,0:T(8,128)}) custom-call(bf16[256,1024]{1,0:T(8,128)(2,1)} %bitcast.9, bf16[256,1024]{1,0:T(8,128)(2,1)} %bitcast.10, bf16[256,1024]{1,0:T(8,128)(2,1)} %bitcast.11, bf16[256,1024]{1,0:T(8,128)(2,1)} %bitcast.12, ...), custom_call_target="tpu_custom_call" | custom-call | tf_op jit(solution)/shard_map/fused/pallas_call | solution.py:384
  119.8 0.0 copy-start.1
  119.8 1.9 %copy.15 = bf16[1,1,256,1024]{3,2,1,0:T(8,128)(2,1)} copy(bf16[1,1,256,1024]{3,2,1,0:T(8,128)(2,1)} %bitcast.15) | data formatting | bytes 1048576
  121.8 0.0 copy-done.1
  121.8 0.0 copy-start
  121.8 0.8 copy.16
  122.6 0.4 copy-done
  123.0 0.0 copy-start.2
  123.0 0.8 copy.17
  123.8 0.3 copy-done.2
  124.1 0.7 copy.18
Async XLA Ops:
  119.8 1.9 %copy-start.1 = (bf16[256,1024]{1,0:T(8,128)(2,1)S(1)}, bf16[256,1024]{1,0:T(8,128)(2,1)}, u32[]{:S(2)}) copy-start(bf16[256,1024]{1,0:T(8,128)(2,1)} %get-tuple-element.9) | copy-start | bytes 1572868
  121.8 1.2 copy-start
  123.0 1.1 copy-start.2

commit v2 on v1

--- a/solution.py
+++ b/solution.py
@@ -15,6 +15,12 @@
 Z_LO = 6
 Z = 12
 NG = 4
+GATHER = (1, 11, 21, 31, 12, 22, 32, 2, 13, 23, 41, 51, 61, 71, 3, 24)
+GATHER += (42, 52, 62, 72, 33, 102, 14, 43, 4, 53, 63, 73, 34, 101, 44, 100)
+GATHER += (54, 64, 74, 104, 103, 105, 106, 107, 200, 202, 203, 201)
+SCATTER = (102, 103, 100, 202, 101, 21, 203, 31, 61, 200, 1, 201, 11, 71, 22, 32)
+SCATTER += (62, 2, 12, 41, 51, 23, 33, 72, 3, 13, 42, 24, 34, 52, 4, 14)
+SCATTER += (63, 73, 43, 302, 303, 53, 300, 301, 64, 74, 44, 54, 306, 307, 304, 305)
 F32 = jnp.float32
 BF16 = jnp.bfloat16
 
@@ -55,12 +61,10 @@
     mx,
     dm,
     gp,
-    gpw,
     gx,
     tm,
     sb,
     rb,
-    za,
     zs,
     zr,
     fb,
@@ -173,7 +177,7 @@
             start(ag(unit, dr, 1, 0))
 
     for g in range(NG):
-        issue(g) if g < 2 else None
+        issue(GATHER[g] // 10)
         start(az(g, zh))
     swap_x = remote(x_hbm, xv.at[1], m_s.at[0], m_r.at[0], sib)
     start(swap_x)
@@ -207,31 +211,30 @@
             dsc[h] = (ss + sa - sa * ss) * (m * SCALE)
             mx[:, h * DH : (h + 1) * DH] = dot(att, vv[:, h * DH : (h + 1) * DH])
 
-    for t in range(1, 2 * NG + 4):
-        if t + 1 < 2 * NG:
-            issue(t + 1)
-        if t == 2:
-            start(shift)
-            xt[:, 0:L] = xv[0].T
-        if t == 5:
-            swap_x.wait_recv()
-            xt[:, L : 2 * L] = xv[1].T
-        unit = t - 4
-        if 0 <= unit < 2 * NG:
+    for n, token in enumerate(GATHER[4:]):
+        kind, unit = divmod(token, 100)
+        if kind == 0:
+            unit, step = divmod(unit, 10)
+            if step == 1:
+                issue(unit)
+            else:
+                for dr in (1, -1):
+                    ag(unit, dr, step - 1, 1).wait_recv()
+                    start(ag(unit, dr, step, 0))
+        elif kind == 1:
             for dr in (1, -1):
                 ag(unit, dr, 4, 1).wait_recv()
             start(ad(unit, c))
-        for step in (3, 2, 1):
-            unit = t - step
-            if 0 <= unit < 2 * NG:
-                for dr in (1, -1):
-                    ag(unit, dr, step, 1).wait_recv()
-                    start(ag(unit, dr, step + 1, 0))
-        g = t - 4 - NG
-        if g >= 0:
-            ad(g, 1 - c).wait_recv()
-            ad(NG + g, 1 - c).wait_recv()
-            forward(g)
+        else:
+            ad(unit, 1 - c).wait_recv()
+            ad(NG + unit, 1 - c).wait_recv()
+            forward(unit)
+        if n == 3:
+            start(shift)
+            xt[:, 0:L] = xv[0].T
+        if n == 7:
+            swap_x.wait_recv()
+            xt[:, L : 2 * L] = xv[1].T
 
     loads[2].wait()
     shift.wait_recv()
@@ -257,118 +260,116 @@
     outs = [pltpu.make_async_copy(ggb, gg_hbm, o_sem.at[0])]
     outs[0].start()
 
-    def swap(h, half):
-        return remote(gp.at[h, half], gx.at[h], ex_s.at[h], ex_r.at[h], sib)
-
-    def backward(h):
-        g, hh = divmod(h, 2)
-        cq = slice(hh * DH, (hh + 1) * DH)
-        ck = slice(256 + hh * DH, 256 + (hh + 1) * DH)
-        ch = slice(h * DH, (h + 1) * DH)
-        datt = dot(dm[:, ch], vv[:, ch], NT).astype(BF16).astype(F32)
-        ds = (datt * dsc[h]).astype(BF16)
-        dq = dot(ds, qk[g, :, ck]).astype(BF16).astype(F32)
-        dq = (dq * dact[g, :, cq]).astype(BF16)
-        dk = dot(ds, qk[g, :, cq], TN).astype(BF16).astype(F32)
-        dk = (dk * dact[g, :, ck]).astype(BF16)
-        gp[h, 0] = dq
-        gp[h, 1] = dk
-        gpw[g, :, cq] = dq
-        gpw[g, :, ck] = dk
-        start(swap(h, 1 - c))
-
-    def term(h):
-        swap(h, 1 - c).wait_recv()
-        full = dot(xt[:, 0:L], gp[h, c]) + dot(xt[:, L : 2 * L], gx[h])
-        tm[h] = full.reshape(Y, 128, DH)
-
-    def rs(h, dr, step):
+    def swap(g, half):
+        return remote(gp.at[g, half], gx.at[g], ex_s.at[g], ex_r.at[g], sib)
+
+    def backward(g):
+        for hh in range(2):
+            h = 2 * g + hh
+            cq = slice(hh * DH, (hh + 1) * DH)
+            ck = slice(256 + hh * DH, 256 + (hh + 1) * DH)
+            ch = slice(h * DH, (h + 1) * DH)
+            datt = dot(dm[:, ch], vv[:, ch], NT).astype(BF16).astype(F32)
+            ds = (datt * dsc[h]).astype(BF16)
+            dq = dot(ds, qk[g, :, ck]).astype(BF16).astype(F32)
+            gp[g, 0, :, cq] = (dq * dact[g, :, cq]).astype(BF16)
+            dk = dot(ds, qk[g, :, cq], TN).astype(BF16).astype(F32)
+            gp[g, 1, :, cq] = (dk * dact[g, :, ck]).astype(BF16)
+        start(swap(g, 1 - c))
+
+    def term(g):
+        swap(g, 1 - c).wait_recv()
+        full = dot(xt[:, 0:L], gp[g, c]) + dot(xt[:, L : 2 * L], gx[g])
+        tm[g] = full.reshape(Y, 2, 64, 256)
+
+    def zz_of(unit):
+        return 1 - zh if unit < NG else zh
+
+    def rs(unit, dr, step):
         di = 0 if dr == 1 else 1
-        src, dst = sb.at[h, di, step - 1], rb.at[h, di, step - 1]
+        src, dst = sb.at[unit, di, step - 1], rb.at[unit, di, step - 1]
         if step == 1:
-            src, dst = src.at[pl.ds(0, 64)], dst.at[pl.ds(0, 64)]
-        return remote(src, dst, rs_s.at[h, di, step - 1], rs_r.at[h, di, step - 1], nxt[dr])
-
-    def rs_send(h, dr, step):
+            src, dst = src.at[pl.ds(0, 32)], dst.at[pl.ds(0, 32)]
+        return remote(src, dst, rs_s.at[unit, di, step - 1], rs_r.at[unit, di, step - 1], nxt[dr])
+
+    def rs_send(unit, dr, step):
         di = 0 if dr == 1 else 1
-        yy = ring(y + dr * (5 - step))
-        lo, hi = (0, 64) if dr == 1 else (64, 0)
+        own = tm.at[unit % NG, ring(y + dr * (5 - step)), zz_of(unit)]
+        lo, hi = (0, 32) if dr == 1 else (32, 0)
         if step == 1:
-            sb[h, di, 0, 0:64] = tm[h, yy, lo : lo + 64].astype(BF16)
+            sb[unit, di, 0, 0:32] = own[lo : lo + 32].astype(BF16)
         elif step == 2:
-            sb[h, di, 1, lo : lo + 64] = (tm[h, yy, lo : lo + 64] + rb[h, di, 0, 0:64].astype(F32)).astype(BF16)
-            sb[h, di, 1, hi : hi + 64] = tm[h, yy, hi : hi + 64].astype(BF16)
+            part = own[lo : lo + 32] + rb[unit, di, 0, 0:32].astype(F32)
+            sb[unit, di, 1, lo : lo + 32] = part.astype(BF16)
+            sb[unit, di, 1, hi : hi + 32] = own[hi : hi + 32].astype(BF16)
         else:
-            sb[h, di, step - 1] = (tm[h, yy] + rb[h, di, step - 2].astype(F32)).astype(BF16)
-        start(rs(h, dr, step))
-
-    def rz(h):
-        return remote(zs.at[h], zr.at[h], rz_s.at[h], rz_r.at[h], opp)
-
-    def rs_end(h):
+            sb[unit, di, step - 1] = (own[...] + rb[unit, di, step - 2].astype(F32)).astype(BF16)
+        start(rs(unit, dr, step))
+
+    def rz(g):
+        return remote(zs.at[g], zr.at[g], rz_s.at[g], rz_r.at[g], opp)
+
+    def col(g, cc):
+        return pl.ds(pl.multiple_of(cc * D + g * 256, 256), 256)
+
+    def rf(g, cc):
+        return remote(fb.at[g, 1 - c], gwb.at[:, col(g, cc)], rf_s.at[g], rf_r.at[g], sib)
+
+    def rs_end(unit):
+        g = unit % NG
         for dr in (1, -1):
-            rs(h, dr, 4).wait_recv()
-        full = tm[h, y] + rb[h, 0, 3].astype(F32) + rb[h, 1, 3].astype(F32)
-        za[h] = full.reshape(2, 64, DH)
-        zs[h] = za[h, 1 - zh].astype(BF16)
-        start(rz(h))
-
-    def col(h, cc):
-        return pl.ds(pl.multiple_of(cc * D + h * DH, DH), DH)
-
-    def rf(h, cc):
-        return remote(fb.at[h, 1 - c], gwb.at[:, col(h, cc)], rf_s.at[h], rf_r.at[h], sib)
-
-    def z_end(h):
-        rz(h).wait_recv()
-        full = za[h, zh] + zr[h].astype(F32)
-        fb[h] = full.reshape(2, 32, DH)
-        start(rf(h, c))
-        gwb[:, col(h, c)] = fb[h, c]
+            rs(unit, dr, 4).wait_recv()
+        full = tm[g, y, zz_of(unit)] + rb[unit, 0, 3].astype(F32) + rb[unit, 1, 3].astype(F32)
+        if unit < NG:
+            zs[g] = full.astype(BF16)
+            start(rz(g))
+        else:
+            rz(g).wait_recv()
+            full = full + zr[g].astype(F32)
+            fb[g] = full.reshape(2, 32, 256)
+            start(rf(g, c))
+            gwb[:, col(g, c)] = fb[g, c]
 
     def grad_values(h):
         ch = slice(h * DH, (h + 1) * DH)
         gvb[:, ch] = dot(at[h], dm[:, ch], TN).astype(BF16)
 
     def grad_inputs(n):
-        acc = dot(gpw[0], wb[0, 2 * n : 2 * n + 2].reshape(256, 512), NT)
-        for g in range(1, NG):
-            acc = acc + dot(gpw[g], wb[g, 2 * n : 2 * n + 2].reshape(256, 512), NT)
+        acc = jnp.zeros((L, 256), F32)
+        for g in range(NG):
+            for half in range(2):
+                wg = wb[g, 2 * n : 2 * n + 2, :, :, :, half * 256 : (half + 1) * 256]
+                acc = acc + dot(gp[g, half], wg.reshape(256, 256), NT)
         gib[:, n * 256 : (n + 1) * 256] = acc.astype(BF16)
 
-    Z_LAG = 3
-    backward(0)
-    for t in range(0, H + 4 + Z_LAG):
-        if t + 1 < H:
-            backward(t + 1)
-        if t < H:
-            term(t)
+    FILL = 17
+    for n, token in enumerate(SCATTER):
+        kind, unit = divmod(token, 100)
+        if kind == 0:
+            unit, step = divmod(unit, 10)
             for dr in (1, -1):
-                rs_send(t, dr, 1)
-        for step in (3, 2, 1):
-            h = t - step
-            if 0 <= h < H:
-                for dr in (1, -1):
-                    rs(h, dr, step).wait_recv()
-                    rs_send(h, dr, step + 1)
-        h = t - 4
-        if 0 <= h < H:
-            rs_end(h)
-        if t < H:
-            grad_values(t)
-            if t == H - 1:
+                if step > 1:
+                    rs(unit, dr, step - 1).wait_recv()
+                rs_send(unit, dr, step)
+        elif kind == 1:
+            backward(unit)
+        elif kind == 2:
+            term(unit)
+        else:
+            rs_end(unit)
+        n -= FILL
+        if 0 <= n < H:
+            grad_values(n)
+            if n == H - 1:
                 outs.append(pltpu.make_async_copy(gvb, gv_hbm, o_sem.at[1]))
                 outs[-1].start()
-        elif t < H + 4:
-            grad_inputs(t - H)
-            if t == H + 3:
+        elif H <= n < H + 4:
+            grad_inputs(n - H)
+            if n == H + 3:
                 outs.append(pltpu.make_async_copy(gib, gi_hbm, o_sem.at[2]))
                 outs[-1].start()
-        h = t - 4 - Z_LAG
-        if 0 <= h < H:
-            z_end(h)
-    for h in range(H):
-        rf(h, 1 - c).wait_recv()
+    for g in range(NG):
+        rf(g, 1 - c).wait_recv()
     outs.append(pltpu.make_async_copy(gwb, gw_hbm, o_sem.at[3]))
     outs[-1].start()
     for cp in sent:
@@ -405,16 +406,14 @@
             pltpu.VMEM((H, L, L), BF16),
             pltpu.VMEM(seq, F32),
             pltpu.VMEM(seq, BF16),
-            pltpu.VMEM((H, 2, L, DH), BF16),
-            pltpu.VMEM((NG, L, 512), BF16),
-            pltpu.VMEM((H, L, DH), BF16),
-            pltpu.VMEM((H, Y, 128, DH), F32),
-            pltpu.VMEM((H, 2, 4, 128, DH), BF16),
-            pltpu.VMEM((H, 2, 4, 128, DH), BF16),
-            pltpu.VMEM((H, 2, 64, DH), F32),
-            pltpu.VMEM((H, 64, DH), BF16),
-            pltpu.VMEM((H, 64, DH), BF16),
-            pltpu.VMEM((H, 2, 32, DH), F32),
+            pltpu.VMEM((NG, 2, L, 256), BF16),
+            pltpu.VMEM((NG, L, 256), BF16),
+            pltpu.VMEM((NG, Y, 2, 64, 256), F32),
+            pltpu.VMEM((2 * NG, 2, 4, 64, 256), BF16),
+            pltpu.VMEM((2 * NG, 2, 4, 64, 256), BF16),
+            pltpu.VMEM((NG, 64, 256), BF16),
+            pltpu.VMEM((NG, 64, 256), BF16),
+            pltpu.VMEM((NG, 2, 32, 256), F32),
             pltpu.VMEM((32, 2 * D), F32),
             pltpu.VMEM(seq, BF16),
             pltpu.VMEM(seq, BF16),
@@ -429,14 +428,14 @@
             dma((2 * NG,)),
             dma((2,)),
             dma((2,)),
-            dma((H,)),
-            dma((H,)),
-            dma((H, 2, 4)),
-            dma((H, 2, 4)),
-            dma((H,)),
-            dma((H,)),
-            dma((H,)),
-            dma((H,)),
+            dma((NG,)),
+            dma((NG,)),
+            dma((2 * NG, 2, 4)),
+            dma((2 * NG, 2, 4)),
+            dma((NG,)),
+            dma((NG,)),
+            dma((NG,)),
+            dma((NG,)),
         ],
         compiler_params=pltpu.CompilerParams(
             collective_id=0, has_side_effects=True, vmem_limit_bytes=60 * 1024 * 1024
@@ -445,10 +444,34 @@
     )(x, v, g, og, lengths, w)
 
 
+def hand_over(*refs):
+    n = len(refs) // 2
+    copies = [
+        pltpu.make_async_copy(refs[i], refs[n + i], refs[-1].at[i]) for i in range(n)
+    ]
+    for cp in copies:
+        cp.start()
+    for cp in copies:
+        cp.wait()
+
+
+def finish(*arrays):
+    any_space = pl.BlockSpec(memory_space=pl.ANY)
+    return pl.pallas_call(
+        hand_over,
+        out_shape=tuple(jax.ShapeDtypeStruct(a.shape, a.dtype) for a in arrays),
+        in_specs=[any_space] * len(arrays),
+        out_specs=(any_space,) * len(arrays),
+        scratch_shapes=[pltpu.SemaphoreType.DMA((len(arrays),))],
+        name="finish",
+    )(*arrays)
+
+
 def on_device(inputs, values, gate_values, out_grad, lengths, qk_weight):
     gi, gv, gg, gw = fused(
         inputs[0, 0], values[0, 0], gate_values[0, 0], out_grad[0, 0], lengths, qk_weight[0]
     )
+    gi, gv, gg, gw = finish(gi, gv, gg, gw)
     return (gi[None, None], gv[None, None], gg[None, None], gw[None])
 
 

time: 125 us -> 144 us (1.15)
  Pallas kernels: 119 us -> 143 us
  local copies, waits for them, and re-layouts: 4.95 us -> 0 us
    pallas_call x0 -> x1, Pallas kernels: none -> 56.7 us  [finish(): pl.pallas_call(hand_over, out_shape=tuple((jax.ShapeDtypeStruct(a.shape,...]
    pallas_call x1, Pallas kernels: 119 us -> 86.3 us  [fused(): pl.pallas_call(kernel, out_shape=(jax.ShapeDtypeStruct(seq, BF16), jax.Sh...]
    unnamed x10 -> x0, local copies, waits for them, and re-layouts: 4.95 us -> none
where the time goes in v2:
time: 144 us
  Pallas kernels  143 us (99%)
    pallas_call x1, Pallas kernels, fused(): pl.pallas_call(kernel, out_shape=(jax.ShapeDtypeStruct(seq, BF16), jax.Sh...  86.3 us
    pallas_call x1, Pallas kernels, finish(): pl.pallas_call(hand_over, out_shape=tuple((jax.ShapeDtypeStruct(a.shape,...  56.7 us

profile of v2, /device:TPU:1, one launch (start us, length us, event | category | flops | bytes accessed | tf_op | source)
XLA Modules:
  0.0 144.3 jit_solution(7980813480450980970)
XLA Ops:
  1.3 86.3 %fused.1 = (bf16[256,1024]{1,0:T(8,128)(2,1)}, bf16[256,1024]{1,0:T(8,128)(2,1)}, bf16[256,1024]{1,0:T(8,128)(2,1)}, f32[32,2048]{1,0:T(8,128)}) custom-call(bf16[256,1024]{1,0:T(8,128)(2,1)} %bitcast.9, bf16[256,1024]{1,0:T(8,128)(2,1)} %bitcast.10, bf16[256,1024]{1,0:T(8,128)(2,1)} %bitcast.11, bf16[256,1024]{1,0:T(8,128)(2,1)} %bitcast.12, ...), custom_call_target="tpu_custom_call" | custom-call | tf_op jit(solution)/shard_map/fused/pallas_call | solution.py:385
  87.6 56.7 %finish.1 = (bf16[256,1024]{1,0:T(8,128)(2,1)}, bf16[256,1024]{1,0:T(8,128)(2,1)}, bf16[256,1024]{1,0:T(8,128)(2,1)}, f32[32,2048]{1,0:T(8,128)}) custom-call(bf16[256,1024]{1,0:T(8,128)(2,1)} %get-tuple-element.12.refs_0_, bf16[256,1024]{1,0:T(8,128)(2,1)} %get-tuple-element.13.refs_1_, bf16[256,1024]{1,0:T(8,128)(2,1)} %get-tuple-element.14.refs_2_, ...), custom_call_target="tpu_custom_call" | custom-call | tf_op jit(solution)/shard_map/finish/pallas_call | solution.py:460

commit v3 on v2

--- a/solution.py
+++ b/solution.py
@@ -1,3 +1,5 @@
+import functools
+
 import jax
 import jax.numpy as jnp
 from jax import lax
@@ -177,8 +179,9 @@
             start(ag(unit, dr, 1, 0))
 
     for g in range(NG):
-        issue(GATHER[g] // 10)
         start(az(g, zh))
+    for token in GATHER[:NG]:
+        issue(token // 10)
     swap_x = remote(x_hbm, xv.at[1], m_s.at[0], m_r.at[0], sib)
     start(swap_x)
     shift = remote(og_hbm, ct, m_s.at[1], m_r.at[1], behind)
@@ -238,24 +241,23 @@
 
     loads[2].wait()
     shift.wait_recv()
-    RB = 32
+    RB = 64
 
     @pl.loop(0, L // RB)
     def _(i):
         sl = pl.ds(pl.multiple_of(i * RB, RB), RB)
         mixed = mx[sl, :]
-        cen = mixed - jnp.sum(mixed, axis=-1, keepdims=True) * (1.0 / D)
-        var = jnp.sum(cen * cen, axis=-1, keepdims=True) * (1.0 / D)
-        r = lax.rsqrt(var + 1e-05)
-        normed = cen * r
         row = lax.broadcasted_iota(jnp.int32, (RB, 1), 0) + i * RB
         live = jnp.where(row < length, 1.0, 0.0)
         cot = ct[sl, :].astype(F32) * live
-        ggb[sl, :] = (cot * normed).astype(BF16)
         dn = cot * gt[sl, :].astype(F32)
         m1 = jnp.sum(dn, axis=-1, keepdims=True) * (1.0 / D)
-        m2 = jnp.sum(dn * normed, axis=-1, keepdims=True) * (1.0 / D)
-        dm[sl, :] = (r * (dn - m1 - normed * m2)).astype(BF16)
+        cen = mixed - jnp.sum(mixed, axis=-1, keepdims=True) * (1.0 / D)
+        var = jnp.sum(cen * cen, axis=-1, keepdims=True) * (1.0 / D)
+        m2 = jnp.sum(dn * cen, axis=-1, keepdims=True) * (1.0 / D)
+        r = lax.rsqrt(var + 1e-05)
+        ggb[sl, :] = (cot * (cen * r)).astype(BF16)
+        dm[sl, :] = (r * (dn - m1 - cen * (m2 * r * r))).astype(BF16)
 
     outs = [pltpu.make_async_copy(ggb, gg_hbm, o_sem.at[0])]
     outs[0].start()
@@ -444,25 +446,30 @@
     )(x, v, g, og, lengths, w)
 
 
-def hand_over(*refs):
-    n = len(refs) // 2
-    copies = [
-        pltpu.make_async_copy(refs[i], refs[n + i], refs[-1].at[i]) for i in range(n)
-    ]
-    for cp in copies:
+def hand_over(n, *refs):
+    sources, targets, rooms, sems = refs[:n], refs[n : 2 * n], refs[2 * n : 3 * n], refs[3 * n]
+    reads = [pltpu.make_async_copy(sources[i], rooms[i], sems.at[0, i]) for i in range(n)]
+    writes = [pltpu.make_async_copy(rooms[i], targets[i], sems.at[1, i]) for i in range(n)]
+    for cp in reads:
         cp.start()
-    for cp in copies:
+    for i in range(n):
+        reads[i].wait()
+        writes[i].start()
+    for cp in writes:
         cp.wait()
 
 
 def finish(*arrays):
+    n = len(arrays)
     any_space = pl.BlockSpec(memory_space=pl.ANY)
     return pl.pallas_call(
-        hand_over,
+        functools.partial(hand_over, n),
         out_shape=tuple(jax.ShapeDtypeStruct(a.shape, a.dtype) for a in arrays),
-        in_specs=[any_space] * len(arrays),
-        out_specs=(any_space,) * len(arrays),
-        scratch_shapes=[pltpu.SemaphoreType.DMA((len(arrays),))],
+        in_specs=[any_space] * n,
+        out_specs=(any_space,) * n,
+        scratch_shapes=[pltpu.VMEM(a.shape, a.dtype) for a in arrays]
+        + [pltpu.SemaphoreType.DMA((2, n))],
+        compiler_params=pltpu.CompilerParams(vmem_limit_bytes=60 * 1024 * 1024),
         name="finish",
     )(*arrays)
 

time: 144 us -> 88.9 us (0.62)
  Pallas kernels: 143 us -> 87.4 us
    pallas_call x1, Pallas kernels: 56.7 us -> 2.33 us  [finish(): pl.pallas_call(functools.partial(hand_over, n), out_shape=tuple((jax.Shap...]
where the time goes in v3:
time: 88.9 us; the launch traced here: 88.7 us
  Pallas kernels  87.4 us (98%)
  between operations  1.29 us (1%)
    pallas_call x1, Pallas kernels, fused(): pl.pallas_call(kernel, out_shape=(jax.ShapeDtypeStruct(seq, BF16), jax.Sh...  85.1 us
    pallas_call x1, Pallas kernels, finish(): pl.pallas_call(functools.partial(hand_over, n), out_shape=tuple((jax.Shap...  2.33 us

profile of v3, /device:TPU:1, one launch (start us, length us, event | category | flops | bytes accessed | tf_op | source)
XLA Modules:
  0.0 88.7 jit_solution(13069560279819394548)
XLA Ops:
  1.3 85.1 %fused.1 = (bf16[256,1024]{1,0:T(8,128)(2,1)}, bf16[256,1024]{1,0:T(8,128)(2,1)}, bf16[256,1024]{1,0:T(8,128)(2,1)}, f32[32,2048]{1,0:T(8,128)}) custom-call(bf16[256,1024]{1,0:T(8,128)(2,1)} %bitcast.9, bf16[256,1024]{1,0:T(8,128)(2,1)} %bitcast.10, bf16[256,1024]{1,0:T(8,128)(2,1)} %bitcast.11, bf16[256,1024]{1,0:T(8,128)(2,1)} %bitcast.12, ...), custom_call_target="tpu_custom_call" | custom-call | tf_op jit(solution)/shard_map/fused/pallas_call | solution.py:387
  86.4 2.3 %finish.1 = (bf16[256,1024]{1,0:T(8,128)(2,1)}, bf16[256,1024]{1,0:T(8,128)(2,1)}, bf16[256,1024]{1,0:T(8,128)(2,1)}, f32[32,2048]{1,0:T(8,128)}) custom-call(bf16[256,1024]{1,0:T(8,128)(2,1)} %get-tuple-element.12.refs_0_, bf16[256,1024]{1,0:T(8,128)(2,1)} %get-tuple-element.13.refs_1_, bf16[256,1024]{1,0:T(8,128)(2,1)} %get-tuple-element.14.refs_2_, ...), custom_call_target="tpu_custom_call" | custom-call | tf_op jit(solution)/shard_map/finish/pallas_call | solution.py:465

commit v4 on v3

--- a/solution.py
+++ b/solution.py
@@ -17,9 +17,9 @@
 Z_LO = 6
 Z = 12
 NG = 4
-GATHER = (1, 11, 21, 31, 12, 22, 32, 2, 13, 23, 41, 51, 61, 71, 3, 24)
-GATHER += (42, 52, 62, 72, 33, 102, 14, 43, 4, 53, 63, 73, 34, 101, 44, 100)
-GATHER += (54, 64, 74, 104, 103, 105, 106, 107, 200, 202, 203, 201)
+GATHER = (1, 21, 31, 11, 2, 22, 12, 32, 3, 23, 41, 13, 51, 61, 71, 24)
+GATHER += (42, 33, 52, 62, 72, 4, 43, 102, 14, 53, 63, 73, 34, 44, 101, 100)
+GATHER += (54, 64, 74, 104, 103, 105, 106, 200, 107, 201, 202, 203)
 SCATTER = (102, 103, 100, 202, 101, 21, 203, 31, 61, 200, 1, 201, 11, 71, 22, 32)
 SCATTER += (62, 2, 12, 41, 51, 23, 33, 72, 3, 13, 42, 24, 34, 52, 4, 14)
 SCATTER += (63, 73, 43, 302, 303, 53, 300, 301, 64, 74, 44, 54, 306, 307, 304, 305)
@@ -43,7 +43,7 @@
     v_hbm,
     g_hbm,
     og_hbm,
-    len_ref,
+    len_hbm,
     w_hbm,
     gi_hbm,
     gv_hbm,
@@ -74,6 +74,7 @@
     gib,
     ggb,
     gvb,
+    len_ref,
     l_sem,
     o_sem,
     ag_s,
@@ -137,6 +138,7 @@
         pltpu.make_async_copy(x_hbm, xv.at[0], l_sem.at[8]),
         pltpu.make_async_copy(v_hbm, vv, l_sem.at[9]),
         pltpu.make_async_copy(g_hbm, gt, l_sem.at[10]),
+        pltpu.make_async_copy(len_hbm, len_ref, l_sem.at[11]),
     ]
     for cp in loads:
         cp.start()
@@ -188,6 +190,7 @@
 
     rows = lax.broadcasted_iota(jnp.int32, (L, L), 0)
     cols = lax.broadcasted_iota(jnp.int32, (L, L), 1)
+    loads[3].wait()
     length = len_ref[0, 0]
     mask[...] = jnp.where((cols <= rows) & (rows < length), 1.0, 0.0)
     loads[0].wait()
@@ -344,6 +347,11 @@
                 acc = acc + dot(gp[g, half], wg.reshape(256, 256), NT)
         gib[:, n * 256 : (n + 1) * 256] = acc.astype(BF16)
 
+    def drain(keep):
+        while len(sent) > keep:
+            sent.pop(0).wait_send()
+
+    gathered = len(sent)
     FILL = 17
     for n, token in enumerate(SCATTER):
         kind, unit = divmod(token, 100)
@@ -359,6 +367,10 @@
             term(unit)
         else:
             rs_end(unit)
+        if n == FILL - 1:
+            drain(len(sent) - gathered)
+        if n == len(SCATTER) - 6:
+            drain(28)
         n -= FILL
         if 0 <= n < H:
             grad_values(n)
@@ -392,7 +404,7 @@
             jax.ShapeDtypeStruct(seq, BF16),
             jax.ShapeDtypeStruct((32, 2 * D), F32),
         ),
-        in_specs=[any_space] * 4 + [pl.BlockSpec(memory_space=pltpu.SMEM), any_space],
+        in_specs=[any_space] * 6,
         out_specs=(any_space,) * 4,
         scratch_shapes=[
             pltpu.VMEM((NG, Y, 2, 2, 32, 512), BF16),
@@ -420,7 +432,8 @@
             pltpu.VMEM(seq, BF16),
             pltpu.VMEM(seq, BF16),
             pltpu.VMEM(seq, BF16),
-            dma((11,)),
+            pltpu.SMEM((1, 1), jnp.int32),
+            dma((12,)),
             dma((4,)),
             dma((2 * NG, 2, 4)),
             dma((2 * NG, 2, 4)),

time: 88.9 us -> 88.5 us (level)
  no operation moved by 1% of the time
where the time goes in v4:
time: 88.5 us; the launch traced here: 88.3 us
  Pallas kernels  87 us (98%)
  between operations  1.29 us (1%)
    pallas_call x1, Pallas kernels, fused(): pl.pallas_call(kernel, out_shape=(jax.ShapeDtypeStruct(seq, BF16), jax.Sh...  84.7 us
    pallas_call x1, Pallas kernels, finish(): pl.pallas_call(functools.partial(hand_over, n), out_shape=tuple((jax.Shap...  2.33 us

profile of v4, /device:TPU:1, one launch (start us, length us, event | category | flops | bytes accessed | tf_op | source)
XLA Modules:
  0.0 88.3 jit_solution(5859161266789703696)
XLA Ops:
  1.3 84.7 %fused.1 = (bf16[256,1024]{1,0:T(8,128)(2,1)}, bf16[256,1024]{1,0:T(8,128)(2,1)}, bf16[256,1024]{1,0:T(8,128)(2,1)}, f32[32,2048]{1,0:T(8,128)}) custom-call(bf16[256,1024]{1,0:T(8,128)(2,1)} %bitcast.9, bf16[256,1024]{1,0:T(8,128)(2,1)} %bitcast.10, bf16[256,1024]{1,0:T(8,128)(2,1)} %bitcast.11, bf16[256,1024]{1,0:T(8,128)(2,1)} %bitcast.12, ...), custom_call_target="tpu_custom_call" | custom-call | tf_op jit(solution)/shard_map/fused/pallas_call | solution.py:399
  86.0 2.3 %finish.1 = (bf16[256,1024]{1,0:T(8,128)(2,1)}, bf16[256,1024]{1,0:T(8,128)(2,1)}, bf16[256,1024]{1,0:T(8,128)(2,1)}, f32[32,2048]{1,0:T(8,128)}) custom-call(bf16[256,1024]{1,0:T(8,128)(2,1)} %get-tuple-element.12.refs_0_, bf16[256,1024]{1,0:T(8,128)(2,1)} %get-tuple-element.13.refs_1_, bf16[256,1024]{1,0:T(8,128)(2,1)} %get-tuple-element.14.refs_2_, ...), custom_call_target="tpu_custom_call" | custom-call | tf_op jit(solution)/shard_map/finish/pallas_call | solution.py:478
